TPU v7x, 32 devices: a whole 2x2x4 slice. The times are simulated.
32 devices in a mesh: group: 4 (over x, core), replica: 8 (over z, y).
Axes of the slice: x: 2, y: 2, z: 4, core: 2. Of those that a mesh axis runs over, the one named last changes fastest.
Arguments:
- tokens: bfloat16 [16, 1024, 384], P('replica', 'group'), may hold values from -6 to 6
- cotangent: bfloat16 [16, 1024, 384], P('replica', 'group'), may hold values from -6 to 6
- weight: float32 [1774592], P('group'), may hold values from -1.6329932 to 1.6329932
- momentum: float32 [1774592], P('group'), may hold values from -40 to 40
- average: float32 [1774592], P('group'), may hold values from -1.6329932 to 1.6329932
- rate: float32 [1], replicated, may hold values from 0.00015625 to 0.000625
- step: int32 [1], replicated, may hold values from 1 to 20
Outputs:
- output: bfloat16 [16, 1024, 384], P('replica', 'group')
- grad_tokens: bfloat16 [16, 1024, 384], P('replica', 'group')
- grad: float32 [1774592], P('group')
- momentum_new: float32 [1774592], P('group')
- average_new: float32 [1774592], P('group')
- weight_new: float32 [1774592], P('group')
- weight_copy: bfloat16 [1774592], P('group')
All inputs are finite; a program needn't handle non-finite values.
Results may differ from a plain program's by a relative error of at most 0.013.
The roundings to bfloat16 on the way count: a program that leaves them out, or rounds other values in their place, can miss the bound.
Values may be sent and summed in bfloat16 or wider, within the bound.
No kernel may reach another device: no remote copies, remote signals or barrier semaphores. Data moves between devices by JAX's collectives and lax.ppermute only.
A program may use at most 448 MiB of HBM per device.

v0:
```python
from functools import partial
import jax
import jax.numpy as jnp
from jax import lax
from jax.sharding import PartitionSpec as P

D = 384
H = 6
DH = 64
FF = 1536
EPSILON = 1e-06
MOMENT = 0.9
DECAY_MAX = 0.999
INV_ROOT_TWO = 0.7071067811865476
INV_ROOT_TAU = 0.3989422804014327


def split_params(flat_vec):
    layout = (
        (D * 3 * D, (D, 3 * D)),
        (D * D, (D, D)),
        (D * FF, (D, FF)),
        (FF * D, (FF, D)),
        (D, (D,)),
        (D, (D,)),
        (3 * D, (3 * D,)),
        (DH, (DH,)),
        (DH, (DH,)),
        (D, (D,)),
        (D, (D,)),
        (D, (D,)),
        (FF, (FF,)),
        (D, (D,)),
    )
    pieces = []
    offset = 0
    for seg_len, seg_shape in layout:
        pieces.append(flat_vec[offset : offset + seg_len].reshape(seg_shape))
        offset = offset + seg_len
    return tuple(pieces)


def norm_forward(values, scale, shift):
    center = values - jnp.mean(values, -1, keepdims=True)
    inv_std = lax.rsqrt(jnp.mean(center * center, -1, keepdims=True) + EPSILON)
    normed = center * inv_std
    return (normed * scale + shift, normed, inv_std)


def norm_backward(grad_out, normed, inv_std, scale):
    grad_norm = grad_out * scale
    inner = jnp.mean(grad_norm * normed, -1, keepdims=True)
    return inv_std * (grad_norm - jnp.mean(grad_norm, -1, keepdims=True) - normed * inner)


def gelu_slope(values):
    return (
        0.5 * (1.0 + lax.erf(values * INV_ROOT_TWO))
        + values * jnp.exp(-0.5 * values * values) * INV_ROOT_TAU
    )


def cross_dot(left, right):
    return lax.dot_general(
        left, right, (((0,), (0,)), ((), ())), preferred_element_type=jnp.float32
    )


def back_dot(left, right):
    return lax.dot_general(
        left, right, (((1,), (1,)), ((), ())), preferred_element_type=jnp.float32
    )


def head_scores(query_b, key_block_rows, row_mask_values, scale_factor):
    query_masked = query_b * row_mask_values
    scores = (
        jnp.einsum("xuc,xlc->xul", query_masked, key_block_rows, preferred_element_type=jnp.float32)
        * scale_factor
    )
    return (query_masked, scores)


def attend_block(operands, masks, scale_factor):
    query_b, key_block_rows, value_block_rows = operands

    def attend_one_head(total, row_mask_values):
        query_masked, scores = head_scores(query_b, key_block_rows, row_mask_values, scale_factor)
        row_peak = jnp.max(scores, -1, keepdims=True)
        raised = jnp.exp(scores - row_peak)
        row_total = jnp.sum(raised, -1, keepdims=True)
        attention_weights = (raised / row_total).astype(jnp.bfloat16)
        part_out = jnp.einsum(
            "cxu,cuw->cxw",
            attention_weights,
            value_block_rows * row_mask_values,
            preferred_element_type=jnp.float32,
        )
        return (total + part_out, (row_peak + jnp.log(row_total))[..., 0])

    start = jnp.zeros(query_b.shape, jnp.float32)
    return lax.scan(attend_one_head, start, masks)


def head_grads(
    query_b, key_block_rows, value_block_rows, grad_b, log_h, inner_h, row_mask_values, scale_factor
):
    query_masked, scores = head_scores(query_b, key_block_rows, row_mask_values, scale_factor)
    probs = jnp.exp(scores - log_h[..., None])
    gradient_masked = grad_b * row_mask_values
    grad_probs = jnp.einsum(
        "xuc,xlc->xul", gradient_masked, value_block_rows, preferred_element_type=jnp.float32
    )
    inner_h = jnp.sum(probs * grad_probs, -1)
    score_gradient = (probs * (grad_probs - inner_h[..., None])).astype(jnp.bfloat16)
    return (probs, score_gradient, inner_h, query_masked, gradient_masked)


def local_back(operands, masks, scale_factor):
    query_b, key_block_rows, value_block_rows, grad_b, log_b = operands

    def local_one_head(carry, head_in):
        row_mask_values, log_h = head_in
        probs, score_gradient, inner_h, query_masked, gradient_masked = head_grads(
            query_b,
            key_block_rows,
            value_block_rows,
            grad_b,
            log_h,
            None,
            row_mask_values,
            scale_factor,
        )
        grad_query = (
            jnp.einsum(
                "cxu,cuw->cxw",
                score_gradient,
                key_block_rows * row_mask_values,
                preferred_element_type=jnp.float32,
            )
            * scale_factor
        )
        grad_key = (
            jnp.einsum(
                "fji,fjp->fip", score_gradient, query_masked, preferred_element_type=jnp.float32
            )
            * scale_factor
        )
        grad_value = jnp.einsum(
            "fji,fjp->fip",
            probs.astype(jnp.bfloat16),
            gradient_masked,
            preferred_element_type=jnp.float32,
        )
        return ((carry[0] + grad_query, carry[1] + grad_key, carry[2] + grad_value), None)

    start = (
        jnp.zeros(query_b.shape, jnp.float32),
        jnp.zeros(key_block_rows.shape, jnp.float32),
        jnp.zeros(key_block_rows.shape, jnp.float32),
    )
    totals, unused = lax.scan(local_one_head, start, (masks, log_b))
    return totals


def per_device(tokens, cotangent, weight, momentum, average, rate, step):
    image_count, own_len, width = tokens.shape
    row_count = image_count * own_len
    scale_factor = DH ** (-0.5)
    pair_size = 2
    head_masks = (
        lax.broadcasted_iota(jnp.int32, (H, width), 1) // DH
        == lax.broadcasted_iota(jnp.int32, (H, width), 0)
    ).astype(jnp.bfloat16)

    def in_blocks(array):
        return array.reshape((image_count // pair_size, pair_size) + array.shape[1:])

    def unblock(array):
        return array.reshape((image_count,) + array.shape[2:])

    shard_low = weight.astype(jnp.bfloat16)
    gathered = lax.all_gather(shard_low, "group", axis=0, tiled=True)
    (
        w_qkv,
        w_out,
        w_fc1,
        w_fc2,
        g_one,
        b_one,
        b_qkv,
        g_query,
        g_key,
        b_out,
        g_two,
        b_two,
        b_fc1,
        b_fc2,
    ) = split_params(gathered)
    (
        gain_one,
        bias_one,
        bias_qkv,
        gain_query,
        gain_key,
        bias_out,
        gain_two,
        bias_two,
        bias_fc1,
        bias_fc2,
    ) = tuple(
        (
            member.astype(jnp.float32)
            for member in (g_one, b_one, b_qkv, g_query, g_key, b_out, g_two, b_two, b_fc1, b_fc2)
        )
    )
    resid_in = tokens.astype(jnp.float32).reshape(row_count, width)
    ln_one_out, normed_one, inv_one = norm_forward(resid_in, gain_one, bias_one)
    act_one = ln_one_out.astype(jnp.bfloat16)
    qkv_full = jnp.dot(act_one, w_qkv, preferred_element_type=jnp.float32) + bias_qkv
    head_shape = (row_count, H, DH)
    query_pre = qkv_full[:, :width].reshape(head_shape)
    key_pre = qkv_full[:, width : 2 * width].reshape(head_shape)
    value_pre = qkv_full[:, 2 * width :]
    query_out, query_normed, query_inv = norm_forward(query_pre, gain_query, 0.0)
    key_out, key_normed, key_inv = norm_forward(key_pre, gain_key, 0.0)
    image_shape = (image_count, own_len, width)
    query_low = query_out.astype(jnp.bfloat16).reshape(image_shape)
    key_low = key_out.astype(jnp.bfloat16).reshape(image_shape)
    value_low = value_pre.astype(jnp.bfloat16).reshape(image_shape)
    key_all, value_all = (
        lax.all_gather(key_low, "group", axis=1, tiled=True),
        lax.all_gather(value_low, "group", axis=1, tiled=True),
    )
    attn_out, log_sum = lax.map(
        partial(attend_block, masks=head_masks, scale_factor=scale_factor),
        (in_blocks(query_low), in_blocks(key_all), in_blocks(value_all)),
    )
    attn_low = unblock(attn_out).reshape(row_count, width).astype(jnp.bfloat16)
    resid_mid = resid_in + jnp.dot(attn_low, w_out, preferred_element_type=jnp.float32) + bias_out
    ln_two_out, normed_two, inv_two = norm_forward(resid_mid, gain_two, bias_two)
    act_two = ln_two_out.astype(jnp.bfloat16)
    hidden_pre = jnp.dot(act_two, w_fc1, preferred_element_type=jnp.float32) + bias_fc1
    hidden_low = jax.nn.gelu(hidden_pre, approximate=False).astype(jnp.bfloat16)
    result = resid_mid + jnp.dot(hidden_low, w_fc2, preferred_element_type=jnp.float32) + bias_fc2
    out_tokens = result.astype(jnp.bfloat16).reshape(tokens.shape)
    regathered = lax.all_gather(shard_low, "group", axis=0, tiled=True)
    back_qkv, back_out, back_fc1, back_fc2 = split_params(regathered)[:4]
    grad_res = cotangent.astype(jnp.float32).reshape(row_count, width)
    grad_mlp = cotangent.reshape(row_count, width)
    d_bias_fc2 = jnp.sum(grad_res, 0)
    d_w_fc2 = cross_dot(hidden_low, grad_mlp)
    grad_pre = (back_dot(grad_mlp, back_fc2) * gelu_slope(hidden_pre)).astype(jnp.bfloat16)
    d_bias_fc1 = jnp.sum(grad_pre.astype(jnp.float32), 0)
    d_w_fc1 = cross_dot(act_two, grad_pre)
    grad_norm_two = back_dot(grad_pre, back_fc1)
    d_gain_two = jnp.sum(grad_norm_two * normed_two, 0)
    d_bias_two = jnp.sum(grad_norm_two, 0)
    grad_mid = grad_res + norm_backward(grad_norm_two, normed_two, inv_two, gain_two)
    grad_proj = grad_mid.astype(jnp.bfloat16)
    d_bias_out = jnp.sum(grad_proj.astype(jnp.float32), 0)
    d_w_out = cross_dot(attn_low, grad_proj)
    grad_attn = back_dot(grad_proj, back_out).astype(jnp.bfloat16).reshape(image_shape)
    grad_q, grad_k_all, grad_v_all = lax.map(
        partial(local_back, masks=head_masks, scale_factor=scale_factor),
        (
            in_blocks(query_low),
            in_blocks(key_all),
            in_blocks(value_all),
            in_blocks(grad_attn),
            log_sum,
        ),
    )
    grad_key, grad_value = (
        lax.psum_scatter(
            unblock(grad_k_all).astype(jnp.bfloat16), "group", scatter_dimension=1, tiled=True
        ).astype(jnp.float32),
        lax.psum_scatter(
            unblock(grad_v_all).astype(jnp.bfloat16), "group", scatter_dimension=1, tiled=True
        ).astype(jnp.float32),
    )
    grad_query_n = unblock(grad_q).reshape(head_shape).astype(jnp.bfloat16).astype(jnp.float32)
    grad_key_n = grad_key.reshape(head_shape).astype(jnp.bfloat16).astype(jnp.float32)
    grad_value_n = grad_value.reshape(row_count, width).astype(jnp.bfloat16).astype(jnp.float32)
    d_gain_query = jnp.sum(grad_query_n * query_normed, (0, 1))
    d_gain_key = jnp.sum(grad_key_n * key_normed, (0, 1))
    grad_query_pre = norm_backward(grad_query_n, query_normed, query_inv, gain_query).reshape(
        row_count, width
    )
    grad_key_pre = norm_backward(grad_key_n, key_normed, key_inv, gain_key).reshape(
        row_count, width
    )
    grad_qkv = jnp.concatenate([grad_query_pre, grad_key_pre, grad_value_n], 1).astype(jnp.bfloat16)
    d_bias_qkv = jnp.sum(grad_qkv.astype(jnp.float32), 0)
    d_w_qkv = cross_dot(act_one, grad_qkv)
    grad_norm_one = back_dot(grad_qkv, back_qkv)
    d_gain_one = jnp.sum(grad_norm_one * normed_one, 0)
    d_bias_one = jnp.sum(grad_norm_one, 0)
    grad_in = grad_mid + norm_backward(grad_norm_one, normed_one, inv_one, gain_one)
    grad_tokens = grad_in.astype(jnp.bfloat16).reshape(tokens.shape)
    local_grad = jnp.concatenate(
        [
            member.reshape(-1)
            for member in (
                d_w_qkv,
                d_w_out,
                d_w_fc1,
                d_w_fc2,
                d_gain_one,
                d_bias_one,
                d_bias_qkv,
                d_gain_query,
                d_gain_key,
                d_bias_out,
                d_gain_two,
                d_bias_two,
                d_bias_fc1,
                d_bias_fc2,
            )
        ]
    )
    group_grad = lax.psum_scatter(
        local_grad.astype(jnp.bfloat16), "group", scatter_dimension=0, tiled=True
    ).astype(jnp.float32)
    grad_total = lax.psum(group_grad, "replica")
    momentum_new = MOMENT * momentum + grad_total
    weight_new = weight - rate[0] * (grad_total + MOMENT * momentum_new)
    step_value = step[0].astype(jnp.float32)
    ema_decay = jnp.minimum(DECAY_MAX, (1.0 + step_value) / (10.0 + step_value))
    average_new = ema_decay * average + (1.0 - ema_decay) * weight_new
    return (
        out_tokens,
        grad_tokens,
        grad_total,
        momentum_new,
        average_new,
        weight_new,
        weight_new.astype(jnp.bfloat16),
    )


def solution(mesh):
    in_specs = (
        P("replica", "group", None),
        P("replica", "group", None),
        P("group"),
        P("group"),
        P("group"),
        P(),
        P(),
    )
    out_specs = (
        P("replica", "group", None),
        P("replica", "group", None),
        P("group"),
        P("group"),
        P("group"),
        P("group"),
        P("group"),
    )
    return jax.shard_map(
        per_device, mesh=mesh, in_specs=in_specs, out_specs=out_specs, check_vma=False
    )
```

profile of v0, /device:TPU:0, one launch (start us, length us, event | category | flops | bytes accessed | tf_op | source)
XLA Modules:
  0.0 935.1 jit_solution(8608521233848531671)
XLA Ops:
  8.8 10.9 %reshape.335 = bf16[1,1,443648]{2,1,0:T(2,128)(2,1)} reshape(bf16[443648]{0:T(1024)(128)(2,1)S(1)} %convert_element_type.177) | data formatting | bytes 1774592
  21.7 51.8 %all-gather.9.cloned.1.call-done = bf16[4,1,443648]{2,1,0:T(2,128)(2,1)} async-done(((bf16[1,1,443648]{2,1,0:T(2,128)(2,1)}), bf16[4,1,443648]{2,1,0:T(2,128)(2,1)}) %all-gather.9.cloned.1.call-update) | async-done | bytes 3549200 | tf_op jit(solution)/shard_map/all_gather | solution.py:183
  73.5 78.3 %reduce.13 = bf16[4,443648]{1,0:T(4,128)(2,1)} reduce(bf16[4,1,443648]{2,1,0:T(2,128)(2,1)} %all-gather.9.cloned.1.call-done, bf16[]{:T(256)} %constant.199), dimensions={1}, to_apply=%all-gather.reduce_sub_computation | reduce | bytes 7098370 | tf_op jit(solution)/shard_map/all_gather | solution.py:183
  151.8 3.3 reshape.336
  159.8 2.9 reshape.314
  172.9 2.5 mul.382
  178.0 3.3 multiply_convert_fusion.1
  182.8 3.2 fusion.70
  186.3 3.2 reshape.322
  196.5 2.9 multiply_convert_fusion.2
  201.5 3.7 copy.71
  205.2 17.9 %all-gather.7.cloned.1.call-done = bf16[2,1024,384]{2,1,0:T(8,128)(2,1)} async-done(((bf16[2,256,384]{2,1,0:T(8,128)(2,1)}), bf16[2,1024,384]{2,1,0:T(8,128)(2,1)}) %all-gather.7.cloned.1.call-update) | async-done | bytes 1572880 | tf_op jit(solution)/shard_map/all_gather | solution.py:233
  223.1 15.4 %while.48 = (s32[]{:T(128)}, f32[2,256,384]{2,1,0:T(8,128)S(1)}, f32[6,2,256]{2,1,0:T(2,128)S(1)}, bf16[6,384]{1,0:T(8,128)(2,1)S(1)}, bf16[2,256,384]{2,1,0:T(8...) while((s32[]{:T(128)}, f32[2,256,384]{2,1,0:T(8,128)S(1)}, ...), condition=%wide.region_9.10_spmd.clone, body=%wide.region_6.9_spmd.clone.sunk | while | flops 811400704 | bytes 17714324 | solution.py:102
  240.0 8.8 fusion.34
  255.1 70.3 %while.49 = (s32[]{:T(128)}, f32[2,256,384]{2,1,0:T(8,128)}, f32[2,1024,384]{2,1,0:T(8,128)}, f32[2,1024,384]{2,1,0:T(8,128)}, bf16[6,384]{1,0:T(8,128)(2,1)S(1)...) while((s32[]{:T(128)}, f32[2,256,384]{2,1,0:T(8,128)}, ...), condition=%wide.region_16.17_spmd.clone, body=%wide.region_14.16_spmd.clone.sunk | while | flops 2023554560 | bytes 92814896 | solution.py:162
  327.5 61.8 %copy.90 = bf16[2,1024,384]{0,2,1:T(8,128)(2,1)} copy(bf16[2,1024,384]{2,1,0:T(8,128)(2,1)S(1)} %convert_element_type.230) | data formatting | bytes 3145728
  389.2 162.7 %reshape.337 = bf16[1024,768]{1,0:T(8,128)(2,1)} reshape(bf16[1024,384,2]{2,1,0:T(8,128)(2,1)} %bitcast.29) | data formatting | bytes 3145728
  570.6 3.5 convolution_convert_fusion.1
  574.1 3.7 reshape.329
  577.8 3.1 multiply_reduce_fusion.4
  586.1 56.0 %reshape.338 = bf16[256,384,2]{2,1,0:T(8,128)(2,1)} reshape(bf16[256,768]{1,0:T(8,128)(2,1)} %reduce-scatter.7.cloned.1.call-done) | data formatting | bytes 786432
  642.1 23.3 %copy.91 = bf16[2,256,384]{1,0,2:T(2,128)(2,1)S(1)} copy(bf16[2,256,384]{0,2,1:T(8,128)(2,1)} %bitcast.123) | data formatting | bytes 786432
  667.9 3.1 multiply_reduce_fusion.3
  680.4 4.6 fusion.57
  686.5 4.0 multiply_reduce_fusion.5
  692.1 2.8 reshape.327
  694.9 50.5 %concatenate.9 = bf16[1774592]{0:T(1024)(128)(2,1)} concatenate(bf16[442368]{0:T(1024)(128)(2,1)} %reshape.327, bf16[147456]{0:T(1024)(128)(2,1)} %reshape.328, bf16[589824]{0:T(1024)(128)(2,1)S(1)} %copy-done.38, bf16[589824]{0:T(1024)(128)(2,1)S(1)} %copy-done.37, bf16[384]{0:T(512)(128)(2,1)} %get-tuple-element.265, bf16[384]{0:T(512)(128)(2,1)} %get-tuple-element.274, ...), dimensions={0} | concatenate | bytes 7098368 | tf_op jit(solution)/shard_map/concatenate | solution.py:301
  747.3 73.6 %all-reduce.6.cloned.1.call-done = bf16[1774592]{0:T(1024)(128)(2,1)} async-done(((bf16[1774592]{0:T(1024)(128)(2,1)}), bf16[1774592]{0:T(1024)(128)(2,1)}) %all-reduce.6.cloned.1.call-update) | async-done | bytes 3549200
  820.9 2.9 dynamic-slice_convert_fusion
  825.2 3.2 fusion.49
  829.6 90.3 %all-reduce.4.cloned.1.call-done = f32[443648]{0:T(1024)} async-done(((f32[443648]{0:T(1024)}), f32[443648]{0:T(1024)}) %all-reduce.4.cloned.1.call-update) | async-done | bytes 1774608 | tf_op jit(solution)/shard_map/psum | solution.py:325
  919.8 4.0 fusion.69
  (436 shorter events, 171.3 us)
Async XLA Ops:
  7.2 66.3 %all-gather.9.cloned.1.call-start = ((), (), s32[]{:S(2)}) async-start(), calls=%async_computation.6 | async-start | bytes 8872960 | tf_op jit(solution)/shard_map/all_gather | solution.py:183
  8.8 11.0 %copy-start.15 = (bf16[2,256,384]{2,1,0:T(8,128)(2,1)S(1)}, bf16[2,256,384]{2,1,0:T(8,128)(2,1)}, u32[]{:S(2)}) copy-start(bf16[2,256,384]{2,1,0:T(8,128)(2,1)} %param.11) | copy-start | bytes 1179652
  19.7 181.8 %all-gather.5.cloned.1.call-start = ((), (), s32[]{:S(2)}) async-start(), calls=%async_computation.2 | async-start | bytes 1966080 | tf_op jit(solution)/shard_map/all_gather | solution.py:232
  155.1 8.7 copy-start.8
  159.8 18.2 %copy-start.60 = (f32[384]{0:T(512)}, f32[384]{0:T(512)S(1)}, u32[]{:S(2)}) copy-start(f32[384]{0:T(512)S(1)} %mul.385) | copy-start | bytes 4612
  165.9 16.0 %copy-start.6 = (f32[512,1152]{1,0:T(8,128)}, f32[512,1152]{1,0:T(8,128)S(1)}, u32[]{:S(2)}) copy-start(f32[512,1152]{1,0:T(8,128)S(1)} %convolution_add_fusion) | copy-start | bytes 7077892
  171.1 6.9 copy-start.54
  178.0 8.0 copy-start.32
  181.4 41.8 %all-gather.7.cloned.1.call-start = ((), (), s32[]{:S(2)}) async-start(), calls=%async_computation.3 | async-start | bytes 1966080 | tf_op jit(solution)/shard_map/all_gather | solution.py:233
  182.7 403.4 %reduce-scatter.7.cloned.1.call-start = ((), (), s32[]{:S(2)}) async-start(), calls=%async_computation.7 | async-start | bytes 1966080
  186.1 9.4 %copy-start.62 = (f32[384]{0:T(512)}, f32[384]{0:T(512)S(1)}, u32[]{:S(2)}) copy-start(f32[384]{0:T(512)S(1)} %mul.377) | copy-start | bytes 4612
  199.4 23.8 %copy-start.51 = (f32[2,256,384]{2,1,0:T(8,128)S(1)}, f32[2,256,384]{2,1,0:T(8,128)}, u32[]{:S(2)}) copy-start(f32[2,256,384]{2,1,0:T(8,128)} %custom-call) | copy-start | bytes 2359300
  223.1 15.6 %copy-start.16 = (bf16[2,256,384]{2,1,0:T(8,128)(2,1)S(1)}, bf16[2,256,384]{2,1,0:T(8,128)(2,1)}, u32[]{:S(2)}) copy-start(bf16[2,256,384]{2,1,0:T(8,128)(2,1)} %param.11) | copy-start | bytes 1179652
  223.1 15.6 %copy-start.67 = (f32[384]{0:T(512)S(1)}, f32[384]{0:T(512)}, u32[]{:S(2)}) copy-start(f32[384]{0:T(512)} %get-tuple-element.321) | copy-start | bytes 4612
  239.4 13.4 %copy-start.21 = (f32[512,384]{1,0:T(8,128)}, f32[512,384]{1,0:T(8,128)S(1)}, u32[]{:S(2)}) copy-start(f32[512,384]{1,0:T(8,128)S(1)} %get-tuple-element.338) | copy-start | bytes 2359300
  240.0 8.8 copy-start.45
  240.0 8.8 copy-start.46
  389.2 163.4 %copy-start.68 = (f32[1,2,2,128]{3,2,1,0:T(2,128)S(1)}, f32[1,2,2,128]{3,2,1,0:T(2,128)}, u32[]{:S(2)}) copy-start(f32[1,2,2,128]{3,2,1,0:T(2,128)} %get-tuple-element.335) | copy-start | bytes 6148
  389.2 164.0 %copy-start.69 = (f32[1,2,2,128]{3,2,1,0:T(2,128)S(1)}, f32[1,2,2,128]{3,2,1,0:T(2,128)}, u32[]{:S(2)}) copy-start(f32[1,2,2,128]{3,2,1,0:T(2,128)} %get-tuple-element.333) | copy-start | bytes 6148
  552.0 133.1 %reduce-scatter.5.cloned.1.call-start = ((), (), s32[]{:S(2)}) async-start(), calls=%async_computation.4 | async-start | bytes 1966080 | tf_op jit(solution)/shard_map/reduce_scatter | solution.py:278
  565.1 255.8 %all-reduce.6.cloned.1.call-start = ((), (), s32[]{:S(2)}) async-start(), calls=%async_computation.8 | async-start | bytes 7098368
  570.6 7.2 copy-start.34
  570.6 7.2 copy-start.35
  574.1 8.1 copy-start.12
  574.1 8.1 copy-start.57
  665.4 6.9 copy-start.10
  665.4 6.9 copy-start.55
  745.4 79.7 %copy-start.23 = (f32[512,384]{1,0:T(8,128)S(1)}, f32[512,384]{1,0:T(8,128)}, u32[]{:S(2)}) copy-start(f32[512,384]{1,0:T(8,128)} %copy-done.21) | copy-start | bytes 2359300
  745.4 79.7 %copy-start.47 = (bf16[1536,384]{1,0:T(8,128)(2,1)S(1)}, bf16[1536,384]{1,0:T(8,128)(2,1)}, u32[]{:S(2)}) copy-start(bf16[1536,384]{1,0:T(8,128)(2,1)} %reshape.322) | copy-start | bytes 3538948
  745.5 79.7 %copy-start.77 = (f32[384]{0:T(512)S(1)}, f32[384]{0:T(512)}, u32[]{:S(2)}) copy-start(f32[384]{0:T(512)} %get-tuple-element.318) | copy-start | bytes 4612
  745.5 174.4 %all-reduce.4.cloned.1.call-start = ((), (), s32[]{:S(2)}) async-start(), calls=%async_computation.5 | async-start | bytes 3555328 | tf_op jit(solution)/shard_map/psum | solution.py:325
  828.4 91.5 %copy-start.20 = (f32[443648]{0:T(1024)S(1)}, f32[443648]{0:T(1024)}, u32[]{:S(2)}) copy-start(f32[443648]{0:T(1024)} %param.13) | copy-start | bytes 5323780
  (94 other events, 243.8 us)
Sparse Core Ops, SparseCore 0:
  19.8 53.6 all-gather.8
  181.5 19.8 all-gather.4
  203.5 19.6 all-gather.6
  552.1 28.0 reduce-scatter.6
  583.1 28.0 reduce-scatter.4
  745.6 75.2 all-reduce.5
  825.1 94.7 all-reduce.3
where the time goes:
time: 944 us; the launch traced here: 935 us
  local copies, waits for them, and re-layouts  471 us (50%)
  waiting for transfers between devices  234 us (25%)
  other arithmetic  128 us (14%)
  matrix products  83.4 us (9%)
  between operations  17.3 us (2%)
    unnamed x164, local copies, waits for them, and re-layouts  332 us
    psum x1, waiting for transfers between devices, per_device(): grad_total = lax.psum(group_grad, 'replica')  90.3 us
    all_gather x1, other arithmetic, per_device(): gathered = lax.all_gather(shard_low, 'group', axis=0, tiled=True)  78.3 us
    unnamed x9, waiting for transfers between devices  73.7 us
    all_gather x1, waiting for transfers between devices, per_device(): gathered = lax.all_gather(shard_low, 'group', axis=0, tiled=True)  51.8 us
    concatenate x1, local copies, waits for them, and re-layouts, per_device(): jnp.concatenate([member.reshape(-1) for member in (d_w_qkv, d_w_out, d_w_...  50.5 us
    while x84, local copies, waits for them, and re-layouts  27.4 us
  transfers between devices with their start and end apart: 7, of which 4 were waited for; matrix products, arithmetic and copies ran while one was open for 17% of the time, Pallas kernels for 0%

commit v1 on v0

--- a/solution.py
+++ b/solution.py
@@ -322,7 +322,11 @@
     group_grad = lax.psum_scatter(
         local_grad.astype(jnp.bfloat16), "group", scatter_dimension=0, tiled=True
     ).astype(jnp.float32)
-    grad_total = lax.psum(group_grad, "replica")
+    grad_total = group_grad
+    for hop in (1, 2, 4):
+        grad_total = grad_total + lax.ppermute(
+            grad_total, "replica", [(dev, dev ^ hop) for dev in range(8)]
+        )
     momentum_new = MOMENT * momentum + grad_total
     weight_new = weight - rate[0] * (grad_total + MOMENT * momentum_new)
     step_value = step[0].astype(jnp.float32)

time: 944 us -> 1010 us (1.070)
  waiting for transfers between devices: 234 us -> 289 us
    ppermute x0 -> x3, waiting for transfers between devices: none -> 146 us  [per_device(): lax.ppermute(grad_total, 'replica', [(dev, dev ^ hop) for dev in range(8)])]
    psum x1 -> x0, waiting for transfers between devices: 90.3 us -> none  [per_device(): grad_total = lax.psum(group_grad, 'replica')]
    unnamed x164 -> x159, local copies, waits for them, and re-layouts: 332 us -> 332 us
    unnamed x9 -> x8, waiting for transfers between devices: 73.7 us -> 73.7 us
  transfers between devices with their start and end apart: 7 -> 9, of which waited for: 4 -> 6; matrix products, arithmetic and copies ran while one was open for 17% -> 16% of each run, Pallas kernels for 0% -> 0%
where the time goes in v1:
time: 1010 us; the launch traced here: 998 us
  local copies, waits for them, and re-layouts  472 us (47%)
  waiting for transfers between devices  289 us (29%)
  other arithmetic  129 us (13%)
  matrix products  84.1 us (8%)
  between operations  17.3 us (2%)
    unnamed x159, local copies, waits for them, and re-layouts  332 us
    ppermute x3, waiting for transfers between devices, per_device(): lax.ppermute(grad_total, 'replica', [(dev, dev ^ hop) for dev in range(8)])  146 us
    all_gather x1, other arithmetic, per_device(): gathered = lax.all_gather(shard_low, 'group', axis=0, tiled=True)  78.3 us
    unnamed x8, waiting for transfers between devices  73.7 us
    all_gather x1, waiting for transfers between devices, per_device(): gathered = lax.all_gather(shard_low, 'group', axis=0, tiled=True)  51.8 us
    concatenate x1, local copies, waits for them, and re-layouts, per_device(): jnp.concatenate([member.reshape(-1) for member in (d_w_qkv, d_w_out, d_w_...  51.2 us
    while x84, local copies, waits for them, and re-layouts  27.5 us
  transfers between devices with their start and end apart: 9, of which 6 were waited for; matrix products, arithmetic and copies ran while one was open for 16% of the time, Pallas kernels for 0%

profile of v1, /device:TPU:0, one launch (start us, length us, event | category | flops | bytes accessed | tf_op | source)
XLA Modules:
  0.0 998.3 jit_solution(30466096800295808)
XLA Ops:
  8.8 10.9 %reshape.335 = bf16[1,1,443648]{2,1,0:T(2,128)(2,1)} reshape(bf16[443648]{0:T(1024)(128)(2,1)S(1)} %convert_element_type.177) | data formatting | bytes 1774592
  21.7 51.8 %all-gather.9.cloned.1.call-done = bf16[4,1,443648]{2,1,0:T(2,128)(2,1)} async-done(((bf16[1,1,443648]{2,1,0:T(2,128)(2,1)}), bf16[4,1,443648]{2,1,0:T(2,128)(2,1)}) %all-gather.9.cloned.1.call-update) | async-done | bytes 3549200 | tf_op jit(solution)/shard_map/all_gather | solution.py:183
  73.5 78.3 %reduce.13 = bf16[4,443648]{1,0:T(4,128)(2,1)} reduce(bf16[4,1,443648]{2,1,0:T(2,128)(2,1)} %all-gather.9.cloned.1.call-done, bf16[]{:T(256)} %constant.199), dimensions={1}, to_apply=%all-gather.reduce_sub_computation | reduce | bytes 7098370 | tf_op jit(solution)/shard_map/all_gather | solution.py:183
  151.8 3.3 reshape.336
  159.7 2.9 reshape.314
  178.0 3.3 multiply_convert_fusion.1
  182.8 3.2 fusion.71
  186.3 3.2 reshape.322
  196.4 2.9 multiply_convert_fusion.2
  201.4 3.7 copy.71
  205.2 18.0 %all-gather.7.cloned.1.call-done = bf16[2,1024,384]{2,1,0:T(8,128)(2,1)} async-done(((bf16[2,256,384]{2,1,0:T(8,128)(2,1)}), bf16[2,1024,384]{2,1,0:T(8,128)(2,1)}) %all-gather.7.cloned.1.call-update) | async-done | bytes 1572880 | tf_op jit(solution)/shard_map/all_gather | solution.py:233
  223.1 15.4 %while.48 = (s32[]{:T(128)}, f32[2,256,384]{2,1,0:T(8,128)S(1)}, f32[6,2,256]{2,1,0:T(2,128)S(1)}, bf16[6,384]{1,0:T(8,128)(2,1)S(1)}, bf16[2,256,384]{2,1,0:T(8...) while((s32[]{:T(128)}, f32[2,256,384]{2,1,0:T(8,128)S(1)}, ...), condition=%wide.region_9.10_spmd.clone, body=%wide.region_6.9_spmd.clone.sunk | while | flops 811400704 | bytes 17714324 | solution.py:102
  240.0 8.8 fusion.34
  255.0 70.4 %while.49 = (s32[]{:T(128)}, f32[2,256,384]{2,1,0:T(8,128)}, f32[2,1024,384]{2,1,0:T(8,128)}, f32[2,1024,384]{2,1,0:T(8,128)}, bf16[6,384]{1,0:T(8,128)(2,1)S(1)...) while((s32[]{:T(128)}, f32[2,256,384]{2,1,0:T(8,128)}, ...), condition=%wide.region_16.17_spmd.clone, body=%wide.region_14.16_spmd.clone.sunk | while | flops 2023554560 | bytes 92814896 | solution.py:162
  327.4 64.0 %copy.90 = bf16[2,1024,384]{0,2,1:T(8,128)(2,1)} copy(bf16[2,1024,384]{2,1,0:T(8,128)(2,1)S(1)} %convert_element_type.230) | data formatting | bytes 3145728
  391.4 162.7 %reshape.337 = bf16[1024,768]{1,0:T(8,128)(2,1)} reshape(bf16[1024,384,2]{2,1,0:T(8,128)(2,1)} %bitcast.29) | data formatting | bytes 3145728
  572.8 3.5 convolution_convert_fusion.1
  576.3 3.7 reshape.329
  580.0 3.1 multiply_reduce_fusion.4
  588.4 56.0 %reshape.338 = bf16[256,384,2]{2,1,0:T(8,128)(2,1)} reshape(bf16[256,768]{1,0:T(8,128)(2,1)} %reduce-scatter.7.cloned.1.call-done) | data formatting | bytes 786432
  644.4 23.3 %copy.91 = bf16[2,256,384]{1,0,2:T(2,128)(2,1)S(1)} copy(bf16[2,256,384]{0,2,1:T(8,128)(2,1)} %bitcast.123) | data formatting | bytes 786432
  670.2 3.1 multiply_reduce_fusion.3
  682.7 4.6 fusion.57
  688.8 4.0 multiply_reduce_fusion.5
  694.4 2.8 reshape.327
  697.2 51.2 %concatenate.9 = bf16[1774592]{0:T(1024)(128)(2,1)} concatenate(bf16[442368]{0:T(1024)(128)(2,1)} %reshape.327, bf16[147456]{0:T(1024)(128)(2,1)} %reshape.328, bf16[589824]{0:T(1024)(128)(2,1)S(1)} %copy-done.36, bf16[589824]{0:T(1024)(128)(2,1)S(1)} %copy-done.35, bf16[384]{0:T(512)(128)(2,1)} %get-tuple-element.265, bf16[384]{0:T(512)(128)(2,1)} %get-tuple-element.274, ...), dimensions={0} | concatenate | bytes 7098368 | tf_op jit(solution)/shard_map/concatenate | solution.py:301
  750.3 73.6 %all-reduce.3.cloned.1.call-done = bf16[1774592]{0:T(1024)(128)(2,1)} async-done(((bf16[1774592]{0:T(1024)(128)(2,1)}), bf16[1774592]{0:T(1024)(128)(2,1)}) %all-reduce.3.cloned.1.call-update) | async-done | bytes 3549200
  827.0 38.9 %collective-permute-done = f32[443648]{0:T(1024)S(1)} collective-permute-done((f32[443648]{0:T(1024)S(1)}, f32[443648]{0:T(1024)S(1)}, u32[]{:S(2)}, u32[]{:S(2)}) %collective-permute-start) | collective-permute-done | bytes 1774624 | tf_op jit(solution)/shard_map/ppermute | solution.py:327
  869.1 38.0 %collective-permute-done.1 = f32[443648]{0:T(1024)S(1)} collective-permute-done((f32[443648]{0:T(1024)S(1)}, f32[443648]{0:T(1024)S(1)}, u32[]{:S(2)}, u32[]{:S(2)}) %collective-permute-start.1) | collective-permute-done | bytes 1774624 | tf_op jit(solution)/shard_map/ppermute | solution.py:327
  911.3 3.8 fusion.49
  916.3 68.9 %collective-permute-done.2 = f32[443648]{0:T(1024)} collective-permute-done((f32[443648]{0:T(1024)S(1)}, f32[443648]{0:T(1024)}, u32[]{:S(2)}, u32[]{:S(2)}) %collective-permute-start.2) | collective-permute-done | bytes 1774624 | tf_op jit(solution)/shard_map/ppermute | solution.py:327
  985.2 4.2 fusion.70
  (436 shorter events, 180.7 us)
Async XLA Ops:
  7.2 66.3 %all-gather.9.cloned.1.call-start = ((), (), s32[]{:S(2)}) async-start(), calls=%async_computation.5 | async-start | bytes 8872960 | tf_op jit(solution)/shard_map/all_gather | solution.py:183
  8.8 11.0 %copy-start.15 = (bf16[2,256,384]{2,1,0:T(8,128)(2,1)S(1)}, bf16[2,256,384]{2,1,0:T(8,128)(2,1)}, u32[]{:S(2)}) copy-start(bf16[2,256,384]{2,1,0:T(8,128)(2,1)} %param.11) | copy-start | bytes 1179652
  19.7 181.7 %all-gather.5.cloned.1.call-start = ((), (), s32[]{:S(2)}) async-start(), calls=%async_computation.2 | async-start | bytes 1966080 | tf_op jit(solution)/shard_map/all_gather | solution.py:232
  155.1 8.7 copy-start.8
  159.7 18.3 %copy-start.58 = (f32[384]{0:T(512)}, f32[384]{0:T(512)S(1)}, u32[]{:S(2)}) copy-start(f32[384]{0:T(512)S(1)} %mul.385) | copy-start | bytes 4612
  165.8 16.1 %copy-start.6 = (f32[512,1152]{1,0:T(8,128)}, f32[512,1152]{1,0:T(8,128)S(1)}, u32[]{:S(2)}) copy-start(f32[512,1152]{1,0:T(8,128)S(1)} %convolution_add_fusion) | copy-start | bytes 7077892
  178.0 8.0 copy-start.30
  181.4 41.8 %all-gather.7.cloned.1.call-start = ((), (), s32[]{:S(2)}) async-start(), calls=%async_computation.3 | async-start | bytes 1966080 | tf_op jit(solution)/shard_map/all_gather | solution.py:233
  182.7 405.7 %reduce-scatter.7.cloned.1.call-start = ((), (), s32[]{:S(2)}) async-start(), calls=%async_computation.6 | async-start | bytes 1966080
  186.1 9.4 copy-start.60
  199.3 23.8 %copy-start.49 = (f32[2,256,384]{2,1,0:T(8,128)S(1)}, f32[2,256,384]{2,1,0:T(8,128)}, u32[]{:S(2)}) copy-start(f32[2,256,384]{2,1,0:T(8,128)} %custom-call) | copy-start | bytes 2359300
  223.1 15.5 %copy-start.16 = (bf16[2,256,384]{2,1,0:T(8,128)(2,1)S(1)}, bf16[2,256,384]{2,1,0:T(8,128)(2,1)}, u32[]{:S(2)}) copy-start(bf16[2,256,384]{2,1,0:T(8,128)(2,1)} %param.11) | copy-start | bytes 1179652
  223.1 15.6 %copy-start.65 = (f32[384]{0:T(512)S(1)}, f32[384]{0:T(512)}, u32[]{:S(2)}) copy-start(f32[384]{0:T(512)} %get-tuple-element.322) | copy-start | bytes 4612
  239.4 13.3 %copy-start.20 = (f32[512,384]{1,0:T(8,128)}, f32[512,384]{1,0:T(8,128)S(1)}, u32[]{:S(2)}) copy-start(f32[512,384]{1,0:T(8,128)S(1)} %get-tuple-element.339) | copy-start | bytes 2359300
  240.0 8.8 copy-start.44
  240.0 8.8 copy-start.45
  391.4 163.4 %copy-start.66 = (f32[1,2,2,128]{3,2,1,0:T(2,128)S(1)}, f32[1,2,2,128]{3,2,1,0:T(2,128)}, u32[]{:S(2)}) copy-start(f32[1,2,2,128]{3,2,1,0:T(2,128)} %get-tuple-element.336) | copy-start | bytes 6148
  391.4 164.0 %copy-start.67 = (f32[1,2,2,128]{3,2,1,0:T(2,128)S(1)}, f32[1,2,2,128]{3,2,1,0:T(2,128)}, u32[]{:S(2)}) copy-start(f32[1,2,2,128]{3,2,1,0:T(2,128)} %get-tuple-element.334) | copy-start | bytes 6148
  554.1 133.2 %reduce-scatter.5.cloned.1.call-start = ((), (), s32[]{:S(2)}) async-start(), calls=%async_computation.4 | async-start | bytes 1966080 | tf_op jit(solution)/shard_map/reduce_scatter | solution.py:278
  567.2 256.6 %all-reduce.3.cloned.1.call-start = ((), (), s32[]{:S(2)}) async-start(), calls=%async_computation.7 | async-start | bytes 7098368
  572.8 7.2 copy-start.32
  572.8 7.2 copy-start.33
  576.3 8.2 copy-start.12
  576.3 8.2 copy-start.55
  667.7 6.9 copy-start.10
  667.7 6.9 copy-start.53
  825.5 40.4 %collective-permute-start = (f32[443648]{0:T(1024)S(1)}, f32[443648]{0:T(1024)S(1)}, u32[]{:S(2)}, u32[]{:S(2)}) collective-permute-start(f32[443648]{0:T(1024)S(1)} %dynamic-slice_convert_fusion), channel_id=1, source_target_pairs={{0,1},{1,0},{2,3},{3,2},{4,5},{5,4},{6,7},{7,6},{8,9},{9,8},{10,11... | collective-permute-start | bytes 5323784 | tf_op jit(solution)/shard_map/ppermute | solution.py:327
  867.6 43.6 %copy-start.75 = (f32[384]{0:T(512)S(1)}, f32[384]{0:T(512)}, u32[]{:S(2)}) copy-start(f32[384]{0:T(512)} %get-tuple-element.319) | copy-start | bytes 4612
  867.6 39.6 %collective-permute-start.1 = (f32[443648]{0:T(1024)S(1)}, f32[443648]{0:T(1024)S(1)}, u32[]{:S(2)}, u32[]{:S(2)}) collective-permute-start(f32[443648]{0:T(1024)S(1)} %fusion.59), channel_id=1, source_target_pairs={{0,2},{1,3},{2,0},{3,1},{4,6},{5,7},{6,4},{7,5},{8,10},{9,11},{10,... | collective-permute-start | bytes 5323784 | tf_op jit(solution)/shard_map/ppermute | solution.py:327
  907.4 77.8 %collective-permute-start.2 = (f32[443648]{0:T(1024)S(1)}, f32[443648]{0:T(1024)}, u32[]{:S(2)}, u32[]{:S(2)}) collective-permute-start(f32[443648]{0:T(1024)S(1)} %add.197), channel_id=1, source_target_pairs={{0,4},{1,5},{2,6},{3,7},{4,0},{5,1},{6,2},{7,3},{8,12},{9,13},{10,... | collective-permute-start | bytes 5323784 | tf_op jit(solution)/shard_map/ppermute | solution.py:327
  911.3 73.9 %copy-start.40 = (f32[443648]{0:T(1024)S(1)}, f32[443648]{0:T(1024)}, u32[]{:S(2)}) copy-start(f32[443648]{0:T(1024)} %param.14) | copy-start | bytes 5323780
  915.1 70.1 %copy-start.19 = (f32[443648]{0:T(1024)S(1)}, f32[443648]{0:T(1024)}, u32[]{:S(2)}) copy-start(f32[443648]{0:T(1024)} %param.13) | copy-start | bytes 5323780
  (94 other events, 251.4 us)
Sparse Core Ops, SparseCore 0:
  19.8 53.6 all-gather.8
  181.5 19.8 all-gather.4
  203.5 19.6 all-gather.6
  554.2 27.9 reduce-scatter.6
  585.2 28.0 reduce-scatter.4
  748.6 75.2 all-reduce.2
